TPU v7x, 256 devices: a whole 4x4x8 slice. The times are simulated.
256 devices in a mesh: row: 8 (over z), col: 16 (over y, x), pan: 2 (over core).
Axes of the slice: x: 4, y: 4, z: 8, core: 2. Of those that a mesh axis runs over, the one named last changes fastest.
Arguments:
- plan_values: bfloat16 [8192, 128, 256], P('row', 'col', 'pan'), may hold values from 0.099609375 to 1
- plan_blocks: int32 [8, 128], P('row', 'col'), may hold values from 0 to 127, as said below
- first_values: bfloat16 [32, 3, 256, 256], P('row'), may hold values from -0.21875 to 0.21875
- first_blocks: int32 [32, 3], P('row'), may hold values from 0 to 3, as said below
- second_values: bfloat16 [128, 6, 256, 256], P('col', None, None, 'pan'), may hold values from -0.15625 to 0.15625
- second_blocks: int32 [128, 6], P('col'), may hold values from 0 to 7, as said below
- weight_first: float32 [8192], P('row'), may hold values from 0.5 to 2
- weight_second: float32 [128, 256], P('col', 'pan'), may hold values from 0.5 to 2
- offset_first: float32 [8192], P('row'), may hold values from -3 to 3
- offset_second: float32 [128, 256], P('col', 'pan'), may hold values from -3 to 3
Outputs:
- new_plan: bfloat16 [8192, 128, 256], P('row', 'col', 'pan')
- scale_first: float32 [8192], P('row')
- scale_second: float32 [128, 256], P('col', 'pan')
Inputs may be any that keep to these rules, and one draw needn't show every extreme that they name: `plan_blocks`: each entry is a slice-B block number; its column panel is the entry // 8. Within the 8 slots of one index of col (aligned groups of the second dimension) no column panel is named more than 2 times, and in every row panel one column panel is named exactly 2 times by every such group. `first_blocks`: block numbers within the row panel of the slice-A block; the 3 entries of a row are distinct. `second_blocks`: block numbers within the column panel of the slice-B block; the 6 entries of a row are distinct.
All inputs are finite; a program needn't handle non-finite values.
Results may differ from a plain program's by a relative error of at most 0.0087.
Values may be sent and summed in bfloat16 or wider, within the bound.
No kernel may reach another device: no remote copies, remote signals or barrier semaphores. Data moves between devices by JAX's collectives and lax.ppermute only.
A program may use at most 128 MiB of HBM per device.

v0:
```python
import jax
import jax.numpy as jnp
from jax import lax
from jax.sharding import PartitionSpec as P

CAP = 2


def first_product(plan_values, first_values, first_blocks):
    tile_count = first_blocks.shape[0]
    block_size = first_values.shape[2]
    slot_count = plan_values.shape[1]
    half_width = plan_values.shape[2]
    row_tiles = plan_values.reshape(tile_count, block_size, slot_count * half_width)
    running = jnp.zeros(row_tiles.shape, jnp.float32)
    for neighbor in range(first_blocks.shape[1]):
        picked = jnp.take(row_tiles, first_blocks[:, neighbor], axis=0)
        running = running + jnp.einsum(
            "iab,ibn->ian", first_values[:, neighbor], picked, preferred_element_type=jnp.float32
        )
    return running.astype(jnp.bfloat16).reshape(tile_count * block_size, slot_count, half_width)


def dispatch(chooser, within_panel, product):
    outgoing = jnp.einsum(
        "dcs,rsh->dcrh", chooser.astype(jnp.bfloat16), product, preferred_element_type=jnp.float32
    ).astype(jnp.bfloat16)
    labels = jnp.sum(chooser.astype(jnp.int32) * (within_panel + 1)[None, None, :], axis=2) - 1
    return (outgoing, labels)


def second_product(dense_plan, second_values, second_blocks):
    blocks_here = second_blocks.shape[0]
    columns = jnp.arange(blocks_here)
    placer = (second_blocks[:, :, None] == columns[None, None, :]).astype(jnp.bfloat16)
    panel_matrix = jnp.einsum(
        "kqbh,kql->kblh", second_values, placer, preferred_element_type=jnp.float32
    ).astype(jnp.bfloat16)
    return jnp.einsum("rkb,kblh->rlh", dense_plan, panel_matrix, preferred_element_type=jnp.float32)


def local(
    plan_values,
    plan_blocks,
    first_values,
    first_blocks,
    second_values,
    second_blocks,
    weight_first,
    weight_second,
    offset_first,
    offset_second,
):
    col_count = lax.axis_size("col")
    blocks_here = second_blocks.shape[0]
    slot_count = plan_values.shape[1]
    block_size = first_values.shape[2]
    panel_rows = plan_values.shape[0]
    plan_width = float(slot_count * col_count * block_size)
    named_blocks = plan_blocks[0]
    target_panel = named_blocks // blocks_here
    within_panel = named_blocks % blocks_here
    same_panel = target_panel[:, None] == target_panel[None, :]
    earlier = jnp.arange(slot_count)[:, None] > jnp.arange(slot_count)[None, :]
    position = jnp.sum((same_panel & earlier).astype(jnp.int32), axis=1)
    chooser = (target_panel[None, None, :] == jnp.arange(col_count)[:, None, None]) & (
        position[None, None, :] == jnp.arange(CAP)[None, :, None]
    )
    product = first_product(plan_values, first_values, first_blocks)
    outgoing, labels = dispatch(chooser, within_panel, product)
    incoming, arrival_ids = (
        lax.all_to_all(outgoing, "col", split_axis=0, concat_axis=0, tiled=True),
        lax.all_to_all(labels, "col", split_axis=0, concat_axis=0, tiled=True),
    )
    item_rows = incoming.shape[2]
    arrivals = incoming.reshape(col_count * CAP, item_rows, incoming.shape[3])
    matcher = (arrival_ids.reshape(-1)[:, None] == jnp.arange(blocks_here)[None, :]).astype(
        jnp.bfloat16
    )
    dense_plan = jnp.einsum(
        "ik,irh->rkh", matcher, arrivals, preferred_element_type=jnp.float32
    ).astype(jnp.bfloat16)
    present = jnp.minimum(jnp.sum(matcher.astype(jnp.float32), axis=0), 1.0)
    gathered = lax.all_gather(dense_plan, "pan", axis=2, tiled=True)
    crossed = second_product(gathered, second_values, second_blocks)
    kernel_values = present[None, :, None] * jnp.exp(
        crossed - offset_first[:, None, None] - offset_second[None]
    )
    row_totals = lax.psum(jnp.sum(kernel_values, axis=(1, 2)), ("col", "pan"))
    scale_first = weight_first * plan_width / row_totals
    weighted = kernel_values * scale_first[:, None, None]
    colsum, counts = lax.psum((jnp.sum(weighted, axis=0), present * float(panel_rows)), "row")
    scale_second = weight_second * counts[:, None] / jnp.where(counts[:, None] > 0, colsum, 1.0)
    new_values = (weighted * scale_second[None]).astype(jnp.bfloat16)
    returned = jnp.einsum(
        "ik,rkh->irh", matcher, new_values, preferred_element_type=jnp.float32
    ).astype(jnp.bfloat16)
    returned = returned.reshape(col_count, CAP, item_rows, returned.shape[2])
    homeward = lax.all_to_all(returned, "col", split_axis=0, concat_axis=0, tiled=True)
    new_plan = jnp.einsum(
        "dcs,dcrh->rsh", chooser.astype(jnp.bfloat16), homeward, preferred_element_type=jnp.float32
    ).astype(jnp.bfloat16)
    return (new_plan, scale_first, scale_second)


def solution(mesh):
    return jax.shard_map(
        local,
        mesh=mesh,
        in_specs=(
            P("row", "col", "pan"),
            P("row", "col"),
            P("row", None, None, None),
            P("row", None),
            P("col", None, None, "pan"),
            P("col", None),
            P("row"),
            P("col", "pan"),
            P("row"),
            P("col", "pan"),
        ),
        out_specs=(P("row", "col", "pan"), P("row"), P("col", "pan")),
        check_vma=False,
    )
```

profile of v0, /device:TPU:2, one launch (start us, length us, event | category | flops | bytes accessed | tf_op | source)
XLA Modules:
  0.0 442.7 jit_solution(4532502949180978923)
XLA Ops:
  7.2 0.0 copy-start
  7.2 0.8 fusion.59
  8.0 0.8 fusion.60
  8.8 0.1 iota_compare_fusion.3
  8.9 0.2 convert_reduce_fusion.1
  9.1 0.1 fusion.47
  9.2 0.7 copy.46
  9.8 7.5 %all-to-all-start = ((s32[16,1,2]{2,1,0:T(1,128)}), s32[16,1,2]{2,1,0:T(1,128)S(1)}, u32[]{:S(2)}, u32[]{:S(2)}) async-start(s32[16,1,2]{2,1,0:T(1,128)} %copy.46), calls=%async_computation | async-start | bytes 16384 | tf_op jit(solution)/shard_map/all_to_all | solution.py:73
  17.3 1.0 slice_reduce_fusion.1
  18.4 4.2 reshape.172
  22.6 3.6 gather_fusion.1
  26.1 3.6 gather_fusion.2
  29.7 3.6 gather_fusion
  33.3 2.8 fusion.20
  36.2 1.0 fusion.22
  37.3 0.5 copy-done.2
  37.8 2.7 fusion.29
  40.5 4.0 copy.53
  44.5 2.2 copy.72
  46.7 5.1 %convolution_convert_fusion.1 = bf16[16,2,1024,128]{3,0,2,1:T(8,128)(2,1)} fusion(bf16[1024,8,128,1]{2,1,0,3:T(8,128)(2,1)S(1)} %bitcast.93, pred[2,8]{1,0:T(4,128)(4,1)S(1)} %iota_compare_fusion.4, pred[16,8]{0,1:T(8,128)(4,1)S(1)} %iota_compare_fusion.3), kind=kOutput, calls=%fused_computation.8 | convolution fusion | flops 71303424 | bytes 10485904 | tf_op jit(solution)/shard_map/dcs,rsh->dcrh/dot_general | solution.py:25
  51.8 8.8 %copy.54 = bf16[16,2,1024,128]{3,2,1,0:T(8,128)(2,1)} copy(bf16[16,2,1024,128]{3,0,2,1:T(8,128)(2,1)} %convolution_convert_fusion.1) | data formatting | bytes 16777216 | tf_op jit(solution)/shard_map/convert_element_type | solution.py:27
  60.6 0.0 all-to-all-done
  60.6 7.2 %all-to-all-start.1 = ((bf16[16,2,1024,128]{3,2,1,0:T(8,128)(2,1)}), bf16[16,2,1024,128]{3,2,1,0:T(8,128)(2,1)}, u32[]{:S(2)}, u32[]{:S(2)}) async-start(bf16[16,2,1024,128]{3,2,1,0:T(8,128)(2,1)} %copy.54), calls=%async_computation.1 | async-start | bytes 16777216 | tf_op jit(solution)/shard_map/all_to_all | solution.py:72
  67.8 0.2 all-gather.2.cloned.1.call-start
  68.1 0.5 broadcast.270
  68.6 0.7 reduce.9
  69.3 0.1 eq.91
  69.3 118.5 %all-to-all-done.1 = bf16[16,2,1024,128]{3,2,1,0:T(8,128)(2,1)} async-done(((bf16[16,2,1024,128]{3,2,1,0:T(8,128)(2,1)}), bf16[16,2,1024,128]{3,2,1,0:T(8,128)(2,1)}, u32[]{:S(2)}, u32[]{:S(2)}) %all-to-all-start.1) | async-done | bytes 8388640 | tf_op jit(solution)/shard_map/all_to_all | solution.py:72
  187.9 9.3 %convert_bitcast_fusion.1 = bf16[1024,8,128]{2,1,0:T(8,128)(2,1)} fusion(bf16[32,1024,128]{2,1,0:T(8,128)(2,1)} %bitcast.10, s32[32]{0:T(128)S(1)} %eq.91), kind=kOutput, calls=%fused_computation.31 | convolution fusion | flops 68157696 | bytes 10485888 | tf_op jit(solution)/shard_map/ik,irh->rkh/dot_general | solution.py:80
  197.2 0.0 all-gather.2.cloned.1.call-update
  197.2 0.0 copy-done
  197.2 0.0 copy-start.7
  197.3 0.0 copy-start.8
  197.3 4.0 convert_bitcast_fusion
  201.2 0.1 convert_reduce_fusion
  201.3 18.2 %all-gather.2.cloned.1.call-done = bf16[1024,8,256]{2,1,0:T(8,128)(2,1)} async-done(((bf16[1024,8,128]{2,1,0:T(8,128)(2,1)}), bf16[1024,8,256]{2,1,0:T(8,128)(2,1)}) %all-gather.2.cloned.1.call-update) | async-done | bytes 4194320 | tf_op jit(solution)/shard_map/all_gather | solution.py:84
  219.5 10.1 %fusion.15 = (f32[1024]{0:T(1024)S(1)}, f32[1024,8,128,1]{2,0,3,1:T(8,128)}) fusion(f32[8,128]{1,0:T(8,128)S(1)} %copy-done.7, f32[1024]{0:T(1024)S(1)} %copy-done.8, f32[8]{0:T(128)S(1)} %get-tuple-element.10, bf16[8,256,8,128]{3,2,1,0:T(8,128)(2,1)} %convert_bitcast_fusion, bf16[1024,8,256]{2,1,0:T(8,128)(2,1)} %all-gather.2.cloned.1.call-done), kind=kOutput, calls=%fused_computation.24 | convolution fusion | flops 4299160576 | bytes 12595232 | tf_op jit(solution)/shard_map/rkb,kblh->rlh/dot_general | solution.py:39
  229.6 62.6 %psum.21 = f32[1024]{0:T(1024)S(1)} all-reduce(f32[1024]{0:T(1024)S(1)} %get-tuple-element.13), channel_id=1, replica_groups=mesh['row'=8,'col'=16,'pan'=2] {'col','pan'}, use_global_device_ids=true, to_apply=%region_4.6 | all-reduce | flops 1024 | bytes 8192 | tf_op jit(solution)/shard_map/psum | solution.py:89
  292.2 0.0 copy-start.5
  292.2 3.3 multiply_reduce_fusion
  295.5 17.7 %all-reduce = (f32[8,128]{1,0:T(8,128)S(1)}, f32[8]{0:T(128)S(1)}) all-reduce(f32[8,128]{1,0:T(8,128)S(1)} %multiply_reduce_fusion, f32[8]{0:T(128)S(1)} %get-tuple-element.9), channel_id=1, replica_groups=mesh['row'=8,'col'=16,'pan'=2] {'row'}, use_global_device_ids=true, to_apply=%region_7.9 | all-reduce | flops 1032 | bytes 8256 | tf_op jit(solution)/shard_map/psum | solution.py:92
  313.2 0.1 select_divide_fusion
  313.3 3.8 multiply_convert_fusion
  317.2 6.3 %convolution_convert_fusion = bf16[32,1024,128]{2,0,1:T(8,128)(2,1)S(1)} fusion(bf16[1024,8,128]{2,0,1:T(8,128)(2,1)S(1)} %multiply_convert_fusion, s32[32]{0:T(128)S(1)} %eq.91), kind=kOutput, calls=%fused_computation.7 | convolution fusion | flops 71303424 | bytes 10485888 | tf_op jit(solution)/shard_map/ik,rkh->irh/dot_general | solution.py:95
  323.5 8.0 %copy.60 = bf16[16,2,1024,128]{3,1,2,0:T(2,128)(2,1)S(1)} copy(bf16[16,2,1024,128]{3,1,0,2:T(2,128)(2,1)S(1)} %bitcast.91) | data formatting | bytes 16777216 | tf_op jit(solution)/shard_map/reshape | solution.py:98
  331.5 0.0 copy-start.1
  331.5 98.3 %all_to_all.16 = bf16[16,2,1024,128]{3,1,2,0:T(2,128)(2,1)S(1)} all-to-all(bf16[16,2,1024,128]{3,1,2,0:T(2,128)(2,1)S(1)} %copy.60), channel_id=1, replica_groups=mesh['row'=8,'col'=16,'pan'=2] {'col'}, dimensions={0} | all-to-all | bytes 16777216 | tf_op jit(solution)/shard_map/all_to_all | solution.py:99
  429.9 6.0 %fusion.32 = bf16[1024,8,128]{2,1,0:T(8,128)(2,1)} fusion(bf16[16,2,1024,128]{3,1,2,0:T(2,128)(2,1)S(1)} %all_to_all.16, pred[2,8]{1,0:T(4,128)(4,1)S(1)} %iota_compare_fusion.4, pred[16,8]{0,1:T(8,128)(4,1)S(1)} %iota_compare_fusion.3), kind=kOutput, calls=%fused_computation.36 | convolution fusion | flops 68157696 | bytes 10485904 | tf_op jit(solution)/shard_map/dcs,dcrh->rsh/dot_general | solution.py:100
  (29 shorter events, 0.1 us)
Async XLA Ops:
  7.2 190.1 %copy-start = (bf16[8,6,256,128]{3,2,1,0:T(8,128)(2,1)S(1)}, bf16[8,6,256,128]{3,2,1,0:T(8,128)(2,1)}, u32[]{:S(2)}) copy-start(bf16[8,6,256,128]{3,2,1,0:T(8,128)(2,1)} %param.16) | copy-start | bytes 9437188
  9.8 50.8 %all-to-all-start = ((s32[16,1,2]{2,1,0:T(1,128)}), s32[16,1,2]{2,1,0:T(1,128)S(1)}, u32[]{:S(2)}, u32[]{:S(2)}) async-start(s32[16,1,2]{2,1,0:T(1,128)} %copy.46), calls=%async_computation | async-start | bytes 16384 | tf_op jit(solution)/shard_map/all_to_all | solution.py:73
  33.3 2.8 copy-start.3
  33.3 2.8 copy-start.4
  36.2 1.6 copy-start.2
  60.6 127.3 %all-to-all-start.1 = ((bf16[16,2,1024,128]{3,2,1,0:T(8,128)(2,1)}), bf16[16,2,1024,128]{3,2,1,0:T(8,128)(2,1)}, u32[]{:S(2)}, u32[]{:S(2)}) async-start(bf16[16,2,1024,128]{3,2,1,0:T(8,128)(2,1)} %copy.54), calls=%async_computation.1 | async-start | bytes 16777216 | tf_op jit(solution)/shard_map/all_to_all | solution.py:72
  67.8 151.7 %all-gather.2.cloned.1.call-start = ((), (), s32[]{:S(2)}) async-start(), calls=%async_computation.3 | async-start | bytes 6291456 | tf_op jit(solution)/shard_map/all_gather | solution.py:84
  187.9 9.4 %copy-start.9 = (s32[8,6]{1,0:T(8,128)S(1)}, s32[8,6]{1,0:T(8,128)}, u32[]{:S(2)}) copy-start(s32[8,6]{1,0:T(8,128)} %param.17) | copy-start | bytes 580
  197.2 22.3 %copy-start.7 = (f32[8,128]{1,0:T(8,128)S(1)}, f32[8,128]{1,0:T(8,128)}, u32[]{:S(2)}) copy-start(f32[8,128]{1,0:T(8,128)} %param.21) | copy-start | bytes 12292
  197.3 22.3 %copy-start.8 = (f32[1024]{0:T(1024)S(1)}, f32[1024]{0:T(1024)}, u32[]{:S(2)}) copy-start(f32[1024]{0:T(1024)} %param.20) | copy-start | bytes 12292
  219.5 72.7 %copy-start.10 = (f32[1024]{0:T(1024)S(1)}, f32[1024]{0:T(1024)}, u32[]{:S(2)}) copy-start(f32[1024]{0:T(1024)} %param.18) | copy-start | bytes 12292
  229.6 83.6 %copy-start.11 = (f32[8,128]{1,0:T(8,128)S(1)}, f32[8,128]{1,0:T(8,128)}, u32[]{:S(2)}) copy-start(f32[8,128]{1,0:T(8,128)} %param.19) | copy-start | bytes 12292
  292.2 24.9 %copy-start.5 = (f32[1024]{0:T(1024)}, f32[1024]{0:T(1024)S(1)}, u32[]{:S(2)}) copy-start(f32[1024]{0:T(1024)S(1)} %multiply_divide_fusion) | copy-start | bytes 12292
  313.3 10.2 %copy-start.6 = (f32[8,128]{1,0:T(8,128)}, f32[8,128]{1,0:T(8,128)S(1)}, u32[]{:S(2)}) copy-start(f32[8,128]{1,0:T(8,128)S(1)} %select_divide_fusion) | copy-start | bytes 12292
  331.5 104.3 %copy-start.1 = (bf16[8,6,256,128]{3,2,1,0:T(8,128)(2,1)S(1)}, bf16[8,6,256,128]{3,2,1,0:T(8,128)(2,1)}, u32[]{:S(2)}) copy-start(bf16[8,6,256,128]{3,2,1,0:T(8,128)(2,1)} %param.16) | copy-start | bytes 9437188
Sparse Core Ops, SparseCore 0:
  197.3 22.1 all-gather.1
where the time goes:
time: 443 us
  blocking collectives  179 us (40%)
  waiting for transfers between devices  137 us (31%)
  matrix products  47.4 us (11%)
  local copies, waits for them, and re-layouts  40.8 us (9%)
  starting transfers between devices  14.9 us (3%)
  between operations  14.3 us (3%)
  other arithmetic  10 us (2%)
    all_to_all x1, waiting for transfers between devices, local(): lax.all_to_all(outgoing, 'col', split_axis=0, concat_axis=0, tiled=True)  119 us
    all_to_all x1, blocking collectives, local(): lax.all_to_all(returned, 'col', split_axis=0, concat_axis=0, tiled=True)  98.3 us
    psum x1, blocking collectives, local(): row_totals = lax.psum(jnp.sum(kernel_values, axis=(1, 2)), ('col', 'pan'))  62.6 us
    all_gather x1, waiting for transfers between devices, local(): gathered = lax.all_gather(dense_plan, 'pan', axis=2, tiled=True)  18.2 us
    psum x1, blocking collectives, local(): lax.psum((jnp.sum(weighted, axis=0), present * float(panel_rows)), 'row')  17.7 us
    gather x3, local copies, waits for them, and re-layouts, first_product(): picked = jnp.take(row_tiles, first_blocks[:, neighbor], axis=0)  10.8 us
    dot_general x1, matrix products, second_product(): jnp.einsum('rkb,kblh->rlh', dense_plan, panel_matrix, preferred_element_t...  10.1 us
    dot_general x1, matrix products, local(): jnp.einsum('ik,irh->rkh', matcher, arrivals, preferred_element_type=jnp.f...  9.33 us
  transfers between devices with their start and end apart: 3, of which 2 were waited for; matrix products, arithmetic and copies ran while one was open for 11% of the time, Pallas kernels for 0%

commit v1 on v0

--- a/solution.py
+++ b/solution.py
@@ -86,7 +86,7 @@
     kernel_values = present[None, :, None] * jnp.exp(
         crossed - offset_first[:, None, None] - offset_second[None]
     )
-    row_totals = lax.psum(jnp.sum(kernel_values, axis=(1, 2)), ("col", "pan"))
+    row_totals = lax.psum(lax.psum(jnp.sum(kernel_values, axis=(1, 2)), "pan"), "col")
     scale_first = weight_first * plan_width / row_totals
     weighted = kernel_values * scale_first[:, None, None]
     colsum, counts = lax.psum((jnp.sum(weighted, axis=0), present * float(panel_rows)), "row")

time: 443 us -> 415 us (0.937)
  blocking collectives: 179 us -> 150 us
    psum x1 -> x2, blocking collectives: 62.6 us -> 39.1 us  [the longest x1 36.6 us: local(): lax.psum(lax.psum(jnp.sum(kernel_values, axis=(1, 2)), 'pan'), 'col')]
    all_to_all x1, blocking collectives: 98.3 us -> 93.6 us  [local(): lax.all_to_all(returned, 'col', split_axis=0, concat_axis=0, tiled=True)]
  transfers between devices with their start and end apart: 3 -> 3, of which waited for: 2 -> 2; matrix products, arithmetic and copies ran while one was open for 11% -> 12% of each run, Pallas kernels for 0% -> 0%
where the time goes in v1:
time: 415 us
  blocking collectives  150 us (36%)
  waiting for transfers between devices  137 us (33%)
  matrix products  47.4 us (11%)
  local copies, waits for them, and re-layouts  40.8 us (10%)
  starting transfers between devices  14.9 us (4%)
  between operations  14.3 us (3%)
  other arithmetic  10 us (2%)
    all_to_all x1, waiting for transfers between devices, local(): lax.all_to_all(outgoing, 'col', split_axis=0, concat_axis=0, tiled=True)  119 us
    all_to_all x1, blocking collectives, local(): lax.all_to_all(returned, 'col', split_axis=0, concat_axis=0, tiled=True)  93.6 us
    psum x1, blocking collectives, local(): lax.psum(lax.psum(jnp.sum(kernel_values, axis=(1, 2)), 'pan'), 'col')  36.6 us
    all_gather x1, waiting for transfers between devices, local(): gathered = lax.all_gather(dense_plan, 'pan', axis=2, tiled=True)  18.2 us
    psum x1, blocking collectives, local(): lax.psum((jnp.sum(weighted, axis=0), present * float(panel_rows)), 'row')  17.7 us
    gather x3, local copies, waits for them, and re-layouts, first_product(): picked = jnp.take(row_tiles, first_blocks[:, neighbor], axis=0)  10.8 us
    dot_general x1, matrix products, second_product(): jnp.einsum('rkb,kblh->rlh', dense_plan, panel_matrix, preferred_element_t...  10.1 us
    dot_general x1, matrix products, local(): jnp.einsum('ik,irh->rkh', matcher, arrivals, preferred_element_type=jnp.f...  9.33 us
  transfers between devices with their start and end apart: 3, of which 2 were waited for; matrix products, arithmetic and copies ran while one was open for 12% of the time, Pallas kernels for 0%

profile of v1, /device:TPU:2, one launch (start us, length us, event | category | flops | bytes accessed | tf_op | source)
XLA Modules:
  0.0 414.6 jit_solution(5951725573588719254)
XLA Ops:
  7.2 0.0 copy-start
  7.2 0.8 fusion.59
  8.0 0.8 fusion.60
  8.8 0.1 iota_compare_fusion.3
  8.9 0.2 convert_reduce_fusion.1
  9.1 0.1 fusion.47
  9.2 0.7 copy.46
  9.8 7.5 %all-to-all-start = ((s32[16,1,2]{2,1,0:T(1,128)}), s32[16,1,2]{2,1,0:T(1,128)S(1)}, u32[]{:S(2)}, u32[]{:S(2)}) async-start(s32[16,1,2]{2,1,0:T(1,128)} %copy.46), calls=%async_computation | async-start | bytes 16384 | tf_op jit(solution)/shard_map/all_to_all | solution.py:73
  17.3 1.0 slice_reduce_fusion.1
  18.4 4.2 %reshape.172 = bf16[4,256,1024]{2,1,0:T(8,128)(2,1)} reshape(bf16[1024,8,128]{2,1,0:T(8,128)(2,1)} %param.12) | data formatting | bytes 4194304 | tf_op jit(solution)/shard_map/reshape | solution.py:14
  22.6 3.6 gather_fusion.1
  26.1 3.6 gather_fusion.2
  29.7 3.6 gather_fusion
  33.3 2.8 fusion.20
  36.2 1.0 fusion.22
  37.3 0.5 copy-done.2
  37.8 2.7 fusion.29
  40.5 4.0 copy.53
  44.5 2.2 copy.72
  46.7 5.1 %convolution_convert_fusion.1 = bf16[16,2,1024,128]{3,0,2,1:T(8,128)(2,1)} fusion(bf16[1024,8,128,1]{2,1,0,3:T(8,128)(2,1)S(1)} %bitcast.93, pred[2,8]{1,0:T(4,128)(4,1)S(1)} %iota_compare_fusion.4, pred[16,8]{0,1:T(8,128)(4,1)S(1)} %iota_compare_fusion.3), kind=kOutput, calls=%fused_computation.8 | convolution fusion | flops 71303424 | bytes 10485904 | tf_op jit(solution)/shard_map/dcs,rsh->dcrh/dot_general | solution.py:25
  51.8 8.8 %copy.54 = bf16[16,2,1024,128]{3,2,1,0:T(8,128)(2,1)} copy(bf16[16,2,1024,128]{3,0,2,1:T(8,128)(2,1)} %convolution_convert_fusion.1) | data formatting | bytes 16777216 | tf_op jit(solution)/shard_map/convert_element_type | solution.py:27
  60.6 0.0 all-to-all-done
  60.6 7.2 %all-to-all-start.1 = ((bf16[16,2,1024,128]{3,2,1,0:T(8,128)(2,1)}), bf16[16,2,1024,128]{3,2,1,0:T(8,128)(2,1)}, u32[]{:S(2)}, u32[]{:S(2)}) async-start(bf16[16,2,1024,128]{3,2,1,0:T(8,128)(2,1)} %copy.54), calls=%async_computation.1 | async-start | bytes 16777216 | tf_op jit(solution)/shard_map/all_to_all | solution.py:72
  67.8 0.2 all-gather.2.cloned.1.call-start
  68.1 0.5 broadcast.270
  68.6 0.7 reduce.9
  69.3 0.1 eq.91
  69.3 118.5 %all-to-all-done.1 = bf16[16,2,1024,128]{3,2,1,0:T(8,128)(2,1)} async-done(((bf16[16,2,1024,128]{3,2,1,0:T(8,128)(2,1)}), bf16[16,2,1024,128]{3,2,1,0:T(8,128)(2,1)}, u32[]{:S(2)}, u32[]{:S(2)}) %all-to-all-start.1) | async-done | bytes 8388640 | tf_op jit(solution)/shard_map/all_to_all | solution.py:72
  187.9 9.3 %convert_bitcast_fusion.1 = bf16[1024,8,128]{2,1,0:T(8,128)(2,1)} fusion(bf16[32,1024,128]{2,1,0:T(8,128)(2,1)} %bitcast.10, s32[32]{0:T(128)S(1)} %eq.91), kind=kOutput, calls=%fused_computation.31 | convolution fusion | flops 68157696 | bytes 10485888 | tf_op jit(solution)/shard_map/ik,irh->rkh/dot_general | solution.py:80
  197.2 0.0 all-gather.2.cloned.1.call-update
  197.2 0.0 copy-start.7
  197.3 0.0 copy-start.8
  197.3 4.0 convert_bitcast_fusion
  201.2 0.1 convert_reduce_fusion
  201.3 18.2 %all-gather.2.cloned.1.call-done = bf16[1024,8,256]{2,1,0:T(8,128)(2,1)} async-done(((bf16[1024,8,128]{2,1,0:T(8,128)(2,1)}), bf16[1024,8,256]{2,1,0:T(8,128)(2,1)}) %all-gather.2.cloned.1.call-update) | async-done | bytes 4194320 | tf_op jit(solution)/shard_map/all_gather | solution.py:84
  219.5 10.1 %fusion.15 = (f32[1024]{0:T(1024)S(1)}, f32[1024,8,128,1]{2,0,3,1:T(8,128)}) fusion(f32[8,128]{1,0:T(8,128)S(1)} %copy-done.7, f32[1024]{0:T(1024)S(1)} %copy-done.8, f32[8]{0:T(128)S(1)} %get-tuple-element.10, bf16[8,256,8,128]{3,2,1,0:T(8,128)(2,1)} %convert_bitcast_fusion, bf16[1024,8,256]{2,1,0:T(8,128)(2,1)} %all-gather.2.cloned.1.call-done), kind=kOutput, calls=%fused_computation.24 | convolution fusion | flops 4299160576 | bytes 12595232 | tf_op jit(solution)/shard_map/rkb,kblh->rlh/dot_general | solution.py:39
  229.6 2.6 psum.28
  232.2 36.6 %psum.29 = f32[1024]{0:T(1024)S(1)} all-reduce(f32[1024]{0:T(1024)S(1)} %psum.28), channel_id=1, replica_groups=mesh['row'=8,'col'=16,'pan'=2] {'col'}, use_global_device_ids=true, to_apply=%region_5.7 | all-reduce | flops 1024 | bytes 8192 | tf_op jit(solution)/shard_map/psum | solution.py:89
  268.8 0.0 copy-start.5
  268.8 3.3 multiply_reduce_fusion
  272.1 17.7 %all-reduce = (f32[8,128]{1,0:T(8,128)S(1)}, f32[8]{0:T(128)S(1)}) all-reduce(f32[8,128]{1,0:T(8,128)S(1)} %multiply_reduce_fusion, f32[8]{0:T(128)S(1)} %get-tuple-element.9), channel_id=1, replica_groups=mesh['row'=8,'col'=16,'pan'=2] {'row'}, use_global_device_ids=true, to_apply=%region_8.10 | all-reduce | flops 1032 | bytes 8256 | tf_op jit(solution)/shard_map/psum | solution.py:92
  289.8 0.1 select_divide_fusion
  289.9 3.8 multiply_convert_fusion
  293.7 6.3 %convolution_convert_fusion = bf16[32,1024,128]{2,0,1:T(8,128)(2,1)S(1)} fusion(bf16[1024,8,128]{2,0,1:T(8,128)(2,1)S(1)} %multiply_convert_fusion, s32[32]{0:T(128)S(1)} %eq.91), kind=kOutput, calls=%fused_computation.7 | convolution fusion | flops 71303424 | bytes 10485888 | tf_op jit(solution)/shard_map/ik,rkh->irh/dot_general | solution.py:95
  300.0 8.0 %copy.60 = bf16[16,2,1024,128]{3,1,2,0:T(2,128)(2,1)S(1)} copy(bf16[16,2,1024,128]{3,1,0,2:T(2,128)(2,1)S(1)} %bitcast.91) | data formatting | bytes 16777216 | tf_op jit(solution)/shard_map/reshape | solution.py:98
  308.1 0.0 copy-start.1
  308.1 93.6 %all_to_all.16 = bf16[16,2,1024,128]{3,1,2,0:T(2,128)(2,1)S(1)} all-to-all(bf16[16,2,1024,128]{3,1,2,0:T(2,128)(2,1)S(1)} %copy.60), channel_id=1, replica_groups=mesh['row'=8,'col'=16,'pan'=2] {'col'}, dimensions={0} | all-to-all | bytes 16777216 | tf_op jit(solution)/shard_map/all_to_all | solution.py:99
  401.8 6.0 %fusion.32 = bf16[1024,8,128]{2,1,0:T(8,128)(2,1)} fusion(bf16[16,2,1024,128]{3,1,2,0:T(2,128)(2,1)S(1)} %all_to_all.16, pred[2,8]{1,0:T(4,128)(4,1)S(1)} %iota_compare_fusion.4, pred[16,8]{0,1:T(8,128)(4,1)S(1)} %iota_compare_fusion.3), kind=kOutput, calls=%fused_computation.36 | convolution fusion | flops 68157696 | bytes 10485904 | tf_op jit(solution)/shard_map/dcs,dcrh->rsh/dot_general | solution.py:100
  (30 shorter events, 0.1 us)
Async XLA Ops:
  7.2 190.1 %copy-start = (bf16[8,6,256,128]{3,2,1,0:T(8,128)(2,1)S(1)}, bf16[8,6,256,128]{3,2,1,0:T(8,128)(2,1)}, u32[]{:S(2)}) copy-start(bf16[8,6,256,128]{3,2,1,0:T(8,128)(2,1)} %param.16) | copy-start | bytes 9437188
  9.8 50.8 %all-to-all-start = ((s32[16,1,2]{2,1,0:T(1,128)}), s32[16,1,2]{2,1,0:T(1,128)S(1)}, u32[]{:S(2)}, u32[]{:S(2)}) async-start(s32[16,1,2]{2,1,0:T(1,128)} %copy.46), calls=%async_computation | async-start | bytes 16384 | tf_op jit(solution)/shard_map/all_to_all | solution.py:73
  33.3 2.8 copy-start.3
  33.3 2.8 copy-start.4
  36.2 1.6 copy-start.2
  60.6 127.3 %all-to-all-start.1 = ((bf16[16,2,1024,128]{3,2,1,0:T(8,128)(2,1)}), bf16[16,2,1024,128]{3,2,1,0:T(8,128)(2,1)}, u32[]{:S(2)}, u32[]{:S(2)}) async-start(bf16[16,2,1024,128]{3,2,1,0:T(8,128)(2,1)} %copy.54), calls=%async_computation.1 | async-start | bytes 16777216 | tf_op jit(solution)/shard_map/all_to_all | solution.py:72
  67.8 151.7 %all-gather.2.cloned.1.call-start = ((), (), s32[]{:S(2)}) async-start(), calls=%async_computation.3 | async-start | bytes 6291456 | tf_op jit(solution)/shard_map/all_gather | solution.py:84
  187.9 9.4 %copy-start.9 = (s32[8,6]{1,0:T(8,128)S(1)}, s32[8,6]{1,0:T(8,128)}, u32[]{:S(2)}) copy-start(s32[8,6]{1,0:T(8,128)} %param.17) | copy-start | bytes 580
  197.2 22.3 %copy-start.7 = (f32[8,128]{1,0:T(8,128)S(1)}, f32[8,128]{1,0:T(8,128)}, u32[]{:S(2)}) copy-start(f32[8,128]{1,0:T(8,128)} %param.21) | copy-start | bytes 12292
  197.3 22.3 %copy-start.8 = (f32[1024]{0:T(1024)S(1)}, f32[1024]{0:T(1024)}, u32[]{:S(2)}) copy-start(f32[1024]{0:T(1024)} %param.20) | copy-start | bytes 12292
  219.5 49.2 %copy-start.10 = (f32[1024]{0:T(1024)S(1)}, f32[1024]{0:T(1024)}, u32[]{:S(2)}) copy-start(f32[1024]{0:T(1024)} %param.18) | copy-start | bytes 12292
  229.6 60.2 %copy-start.11 = (f32[8,128]{1,0:T(8,128)S(1)}, f32[8,128]{1,0:T(8,128)}, u32[]{:S(2)}) copy-start(f32[8,128]{1,0:T(8,128)} %param.19) | copy-start | bytes 12292
  268.8 24.9 %copy-start.5 = (f32[1024]{0:T(1024)}, f32[1024]{0:T(1024)S(1)}, u32[]{:S(2)}) copy-start(f32[1024]{0:T(1024)S(1)} %multiply_divide_fusion) | copy-start | bytes 12292
  289.9 10.2 %copy-start.6 = (f32[8,128]{1,0:T(8,128)}, f32[8,128]{1,0:T(8,128)S(1)}, u32[]{:S(2)}) copy-start(f32[8,128]{1,0:T(8,128)S(1)} %select_divide_fusion) | copy-start | bytes 12292
  308.1 99.6 %copy-start.1 = (bf16[8,6,256,128]{3,2,1,0:T(8,128)(2,1)S(1)}, bf16[8,6,256,128]{3,2,1,0:T(8,128)(2,1)}, u32[]{:S(2)}) copy-start(bf16[8,6,256,128]{3,2,1,0:T(8,128)(2,1)} %param.16) | copy-start | bytes 9437188
Sparse Core Ops, SparseCore 0:
  197.3 22.1 all-gather.1
